TPU v7x, 32 devices: a whole 2x2x4 slice. The times are simulated.
32 devices in a mesh: groups: 2 (over y), sub: 16 (over z, x, core).
Axes of the slice: x: 2, y: 2, z: 4, core: 2. Of those that a mesh axis runs over, the one named last changes fastest.
Arguments:
- samples: bfloat16 [16896, 512], P(('groups', 'sub')), parts along dimension 0, may hold values from -6 to 6
- channel_order: int32 [512], replicated, may hold values from 0 to 511, each once
- merge_table: int32 [9, 3, 256], replicated, may hold values from 0 to 128, as said below
Outputs:
- spectra: float32 [512, 4096], P(('groups', 'sub')), parts along dimension 0
There are 2 independent parts, one for each index of `groups`. A program takes and returns all parts, laid end to end along the dimension named above; an argument that names none is the same for every part. Nothing has to cross between parts.
Inputs may be any that keep to these rules, and one draw needn't show every extreme that they name: `channel_order`: a permutation of the 512 channels. `merge_table`: for level l, entry j is row d = j % 2**(l-1) of merged subband j // 2**(l-1); with C = max(1, 2**(l-2)) and e = 8, entries 0 and 1 lie in [e * (d // (2 e)), e * (d // (2 e)) + min(C, e)), and entry 2 equals entry 0 or entry 0 plus 1.
All inputs are finite; a program needn't handle non-finite values.
Results may differ from a plain program's by a relative error of at most 0.012.
Values may be sent and summed in bfloat16 or wider, within the bound.
A program may use at most 64 MiB of HBM per device.

v0:
```python
import math

import jax
import jax.numpy as jnp
from jax import lax
from jax.sharding import PartitionSpec as P

LOCAL = 5
CH_DEV = 32
SAMPLES = 8192


def from_partner(block, axis, apart):
    count = lax.axis_size(axis)
    route = []
    for low in range(count):
        high = low | 1 << apart
        if high != low and high < count:
            route += [(low, high), (high, low)]
    return lax.ppermute(block, axis, route)


def delay_rows(values, shifts, margin, time_axis):
    length = values.shape[time_axis]
    moved = values
    for bit_num in range(max(1, margin.bit_length())):
        offset = 2**bit_num
        rolled = jnp.pad(moved[:, offset:], ((0, 0), (0, offset)))
        flagged = shifts >> bit_num & 1 == 1
        flagged = flagged[:, None]
        moved = jnp.where(flagged, rolled, moved)
    return moved


def merge_level(current, entries, child_rows, span_rows, time_axis):
    outputs = jnp.arange(entries.shape[1], dtype=jnp.int32)
    starts = 2 * child_rows * (outputs // span_rows)
    lower_rows = jnp.take(current, starts + entries[0], axis=1 - time_axis)
    upper_rows = jnp.take(current, starts + child_rows + entries[1], axis=1 - time_axis)
    moved_rows = delay_rows(upper_rows, entries[2], child_rows, time_axis)
    return (lower_rows.astype(jnp.float32) + moved_rows.astype(jnp.float32)).astype(jnp.bfloat16)


def spectrum(delays, channels):
    row_count = delays.shape[0]
    length = delays.shape[1]
    fold_size = length // 128
    first_index = jnp.arange(fold_size, dtype=jnp.int32)
    lane_index = jnp.arange(128, dtype=jnp.int32)
    half_index = jnp.arange(64, dtype=jnp.int32)
    angle_one = (
        2.0
        * math.pi
        / fold_size
        * (first_index[:, None] * first_index[None, :] % fold_size).astype(jnp.float32)
    )
    cos_one = jnp.cos(angle_one).astype(jnp.bfloat16)
    sin_one = jnp.sin(angle_one).astype(jnp.bfloat16)
    angle_two = (
        2.0
        * math.pi
        / length
        * (first_index[:, None] * lane_index[None, :] % length).astype(jnp.float32)
    )
    twist_cos = jnp.cos(angle_two)
    twist_sin = jnp.sin(angle_two)
    angle_three = (
        2.0 * math.pi / 128 * (lane_index[:, None] * half_index[None, :] % 128).astype(jnp.float32)
    )
    cos_three = jnp.cos(angle_three).astype(jnp.bfloat16)
    sin_three = jnp.sin(angle_three).astype(jnp.bfloat16)
    series = delays.reshape(row_count, fold_size, 128)
    first_re = jnp.einsum("kn,rnm->rkm", cos_one, series, preferred_element_type=jnp.float32)
    first_im = -jnp.einsum("kn,rnm->rkm", sin_one, series, preferred_element_type=jnp.float32)
    twisted_re = (first_re * twist_cos + first_im * twist_sin).astype(jnp.bfloat16)
    twisted_im = (first_im * twist_cos - first_re * twist_sin).astype(jnp.bfloat16)
    out_re = jnp.einsum(
        "rkn,nj->rjk", twisted_re, cos_three, preferred_element_type=jnp.float32
    ) + jnp.einsum("rkn,nj->rjk", twisted_im, sin_three, preferred_element_type=jnp.float32)
    out_im = jnp.einsum(
        "rkn,nj->rjk", twisted_im, cos_three, preferred_element_type=jnp.float32
    ) - jnp.einsum("rkn,nj->rjk", twisted_re, sin_three, preferred_element_type=jnp.float32)
    power = (out_re * out_re + out_im * out_im) / (length * channels)
    return power.reshape(row_count, 64 * fold_size)


def local(samples, channel_order, merge_table):
    owners = lax.axis_size("sub")
    owner_index = lax.axis_index("sub")
    owned_rows = CH_DEV // 2
    quarter = CH_DEV // 4
    window = samples.shape[0]
    channels = samples.shape[1]
    ordered = jnp.take(samples, channel_order, axis=1).T.reshape(owners, CH_DEV, window)
    current = lax.all_to_all(ordered, "sub", split_axis=0, concat_axis=2, tiled=True).reshape(
        CH_DEV, window * owners
    )
    for level_num in range(1, LOCAL + 1):
        entries = lax.dynamic_slice_in_dim(
            merge_table[level_num - 1], owner_index * owned_rows, owned_rows, 1
        )
        current = merge_level(
            current, entries, max(1, 2 ** (level_num - 2)), 2 ** (level_num - 1), 1
        )
    block_index = jnp.zeros((), jnp.int32)
    for bit_num in range(owners.bit_length() - 1):
        level_num = LOCAL + bit_num + 1
        half_bit = owner_index >> bit_num & 1
        block_index = block_index * 2 + half_bit
        span_rows = owned_rows * 2 ** (bit_num + 1)
        child_rows = span_rows // 2
        subband = owner_index >> bit_num + 1
        entries = lax.dynamic_slice_in_dim(
            merge_table[level_num - 1],
            subband * span_rows + owned_rows * block_index,
            owned_rows,
            1,
        )
        kept_rows = lax.dynamic_slice_in_dim(current, half_bit * quarter, quarter, 0)
        sent_rows = lax.dynamic_slice_in_dim(current, (1 - half_bit) * quarter, quarter, 0)
        partner = from_partner(sent_rows, "sub", bit_num)
        row_base = quarter * block_index
        is_low = half_bit == 0
        lower_part = jnp.where(is_low, kept_rows, partner)
        upper_part = jnp.where(is_low, partner, kept_rows)
        lower_rows = jnp.take(lower_part, entries[0] - row_base, axis=0)
        upper_rows = jnp.take(upper_part, entries[1] - row_base, axis=0)
        moved_rows = delay_rows(upper_rows, entries[2], child_rows, 1)
        current = (lower_rows.astype(jnp.float32) + moved_rows.astype(jnp.float32)).astype(
            jnp.bfloat16
        )
    return spectrum(current[:, :SAMPLES], channels)


def solution(mesh):
    in_specs = (P(("groups", "sub"), None), P(), P())
    out_specs = P(("groups", "sub"), None)
    return jax.shard_map(local, mesh=mesh, in_specs=in_specs, out_specs=out_specs, check_vma=False)
```

profile of v0, /device:TPU:0, one launch (start us, length us, event | category | flops | bytes accessed | tf_op | source)
XLA Modules:
  0.0 79.7 jit_solution(5246893528105562320)
XLA Ops:
  0.0 0.8 compare_and_fusion.18
  0.8 1.3 %copy.4 = bf16[528,512]{0,1:T(8,128)(2,1)S(1)} copy(bf16[528,512]{1,0:T(8,128)(2,1)} %param.9) | data formatting | bytes 1081344 | tf_op args[0]
  2.1 2.0 %gather_fusion = bf16[512,528]{1,0:T(8,128)(2,1)S(1)} fusion(bf16[528,512]{0,1:T(8,128)(2,1)S(1)} %copy.4, s32[1024]{0:T(1024)S(1)} %pad_clamp_fusion.18), kind=kCustom, calls=%fused_computation.18 | custom fusion | bytes 1083392 | tf_op jit(solution)/shard_map/jit(_take)/gather | solution.py:94
  4.2 1.0 %broadcast_select_fusion = bf16[512,528]{1,0:T(8,128)(2,1)} fusion(bf16[512,528]{1,0:T(8,128)(2,1)S(1)} %gather_fusion, pred[512]{0:T(512)(128)(4,1)S(1)} %compare_and_fusion.18), kind=kLoop, calls=%fused_computation.29 | loop fusion | flops 270336 | bytes 1081856 | tf_op jit(solution)/shard_map/jit(_take)/select_n | solution.py:94
  5.2 7.4 %all-to-all-start = ((bf16[16,32,528]{2,1,0:T(8,128)(2,1)}), bf16[16,32,528]{2,1,0:T(8,128)(2,1)S(1)}, u32[]{:S(2)}, u32[]{:S(2)}) async-start(bf16[16,32,528]{2,1,0:T(8,128)(2,1)} %bitcast.10), calls=%async_computation | async-start | bytes 1310720 | tf_op jit(solution)/shard_map/all_to_all | solution.py:95
  12.6 0.7 copy-done
  14.3 14.9 %all-to-all-done = bf16[16,32,528]{2,1,0:T(8,128)(2,1)S(1)} async-done(((bf16[16,32,528]{2,1,0:T(8,128)(2,1)}), bf16[16,32,528]{2,1,0:T(8,128)(2,1)S(1)}, u32[]{:S(2)}, u32[]{:S(2)}) %all-to-all-start) | async-done | bytes 540704 | tf_op jit(solution)/shard_map/all_to_all | solution.py:95
  30.0 0.7 gather_fusion.2
  30.7 0.7 gather_fusion.1
  34.5 0.7 gather_fusion.5
  36.0 0.7 gather_fusion.8
  38.5 0.7 gather_fusion.10
  39.2 0.7 gather_fusion.9
  41.5 1.2 %collective-permute-done = bf16[8,8448]{1,0:T(8,128)(2,1)S(1)} collective-permute-done((bf16[8,8448]{1,0:T(8,128)(2,1)S(1)}, bf16[8,8448]{1,0:T(8,128)(2,1)S(1)}, u32[]{:S(2)}, u32[]{:S(2)}) %collective-permute-start) | collective-permute-done | bytes 135200 | tf_op jit(solution)/shard_map/ppermute | solution.py:20
  44.8 0.7 gather_fusion.11
  45.8 1.3 %collective-permute-start.1 = (bf16[8,8448]{1,0:T(8,128)(2,1)S(1)}, bf16[8,8448]{1,0:T(8,128)(2,1)S(1)}, u32[]{:S(2)}, u32[]{:S(2)}) collective-permute-start(bf16[8,8448]{1,0:T(8,128)(2,1)S(1)} %constant_dynamic-slice_fusion.5), channel_id=1, source_target_pairs={{0,2},{2,0},{1,3},{3,1},{4,6},{6,4},{5,7},{7,5},{8,10},{10,8},{9,1... | collective-permute-start | bytes 405512 | tf_op jit(solution)/shard_map/ppermute | solution.py:20
  47.1 4.4 %collective-permute-done.1 = bf16[8,8448]{1,0:T(8,128)(2,1)S(1)} collective-permute-done((bf16[8,8448]{1,0:T(8,128)(2,1)S(1)}, bf16[8,8448]{1,0:T(8,128)(2,1)S(1)}, u32[]{:S(2)}, u32[]{:S(2)}) %collective-permute-start.1) | collective-permute-done | bytes 135200 | tf_op jit(solution)/shard_map/ppermute | solution.py:20
  51.6 0.7 gather_fusion.14
  54.0 0.7 gather_fusion.13
  54.9 2.3 %collective-permute-start.2 = (bf16[8,8448]{1,0:T(8,128)(2,1)S(1)}, bf16[8,8448]{1,0:T(8,128)(2,1)S(1)}, u32[]{:S(2)}, u32[]{:S(2)}) collective-permute-start(bf16[8,8448]{1,0:T(8,128)(2,1)S(1)} %constant_dynamic-slice_fusion.3), channel_id=1, source_target_pairs={{0,4},{4,0},{1,5},{5,1},{2,6},{6,2},{3,7},{7,3},{8,12},{12,8},{9,1... | collective-permute-start | bytes 405512 | tf_op jit(solution)/shard_map/ppermute | solution.py:20
  57.2 3.2 %collective-permute-done.2 = bf16[8,8448]{1,0:T(8,128)(2,1)S(1)} collective-permute-done((bf16[8,8448]{1,0:T(8,128)(2,1)S(1)}, bf16[8,8448]{1,0:T(8,128)(2,1)S(1)}, u32[]{:S(2)}, u32[]{:S(2)}) %collective-permute-start.2) | collective-permute-done | bytes 135200 | tf_op jit(solution)/shard_map/ppermute | solution.py:20
  64.3 2.5 %collective-permute-start.3 = (bf16[8,8448]{1,0:T(8,128)(2,1)S(1)}, bf16[8,8448]{1,0:T(8,128)(2,1)S(1)}, u32[]{:S(2)}, u32[]{:S(2)}) collective-permute-start(bf16[8,8448]{1,0:T(8,128)(2,1)S(1)} %constant_dynamic-slice_fusion.1), channel_id=1, source_target_pairs={{0,8},{8,0},{1,9},{9,1},{2,10},{10,2},{3,11},{11,3},{4,12},{12,4},... | collective-permute-start | bytes 405512 | tf_op jit(solution)/shard_map/ppermute | solution.py:20
  67.0 5.6 %collective-permute-done.3 = bf16[8,8448]{1,0:T(8,128)(2,1)S(1)} collective-permute-done((bf16[8,8448]{1,0:T(8,128)(2,1)S(1)}, bf16[8,8448]{1,0:T(8,128)(2,1)S(1)}, u32[]{:S(2)}, u32[]{:S(2)}) %collective-permute-start.3) | collective-permute-done | bytes 135200 | tf_op jit(solution)/shard_map/ppermute | solution.py:20
  78.8 0.9 %reshape.632 = f32[16,4096]{1,0:T(8,128)} reshape(f32[16,64,64]{2,1,0:T(8,128)S(1)} %fusion.5) | data formatting | bytes 524288 | tf_op jit(solution)/shard_map/reshape | solution.py:84
  (155 shorter events, 22.9 us)
Async XLA Ops:
  0.0 0.8 copy-start.1
  5.2 24.0 %all-to-all-start = ((bf16[16,32,528]{2,1,0:T(8,128)(2,1)}), bf16[16,32,528]{2,1,0:T(8,128)(2,1)S(1)}, u32[]{:S(2)}, u32[]{:S(2)}) async-start(bf16[16,32,528]{2,1,0:T(8,128)(2,1)} %bitcast.10), calls=%async_computation | async-start | bytes 1310720 | tf_op jit(solution)/shard_map/all_to_all | solution.py:95
  12.6 0.8 copy-start
  41.2 1.4 %collective-permute-start = (bf16[8,8448]{1,0:T(8,128)(2,1)S(1)}, bf16[8,8448]{1,0:T(8,128)(2,1)S(1)}, u32[]{:S(2)}, u32[]{:S(2)}) collective-permute-start(bf16[8,8448]{1,0:T(8,128)(2,1)S(1)} %constant_dynamic-slice_fusion.7), channel_id=1, source_target_pairs={{0,1},{1,0},{2,3},{3,2},{4,5},{5,4},{6,7},{7,6},{8,9},{9,8},{10,11... | collective-permute-start | bytes 405512 | tf_op jit(solution)/shard_map/ppermute | solution.py:20
  45.8 5.7 %collective-permute-start.1 = (bf16[8,8448]{1,0:T(8,128)(2,1)S(1)}, bf16[8,8448]{1,0:T(8,128)(2,1)S(1)}, u32[]{:S(2)}, u32[]{:S(2)}) collective-permute-start(bf16[8,8448]{1,0:T(8,128)(2,1)S(1)} %constant_dynamic-slice_fusion.5), channel_id=1, source_target_pairs={{0,2},{2,0},{1,3},{3,1},{4,6},{6,4},{5,7},{7,5},{8,10},{10,8},{9,1... | collective-permute-start | bytes 405512 | tf_op jit(solution)/shard_map/ppermute | solution.py:20
  54.9 5.5 %collective-permute-start.2 = (bf16[8,8448]{1,0:T(8,128)(2,1)S(1)}, bf16[8,8448]{1,0:T(8,128)(2,1)S(1)}, u32[]{:S(2)}, u32[]{:S(2)}) collective-permute-start(bf16[8,8448]{1,0:T(8,128)(2,1)S(1)} %constant_dynamic-slice_fusion.3), channel_id=1, source_target_pairs={{0,4},{4,0},{1,5},{5,1},{2,6},{6,2},{3,7},{7,3},{8,12},{12,8},{9,1... | collective-permute-start | bytes 405512 | tf_op jit(solution)/shard_map/ppermute | solution.py:20
  64.3 8.3 %collective-permute-start.3 = (bf16[8,8448]{1,0:T(8,128)(2,1)S(1)}, bf16[8,8448]{1,0:T(8,128)(2,1)S(1)}, u32[]{:S(2)}, u32[]{:S(2)}) collective-permute-start(bf16[8,8448]{1,0:T(8,128)(2,1)S(1)} %constant_dynamic-slice_fusion.1), channel_id=1, source_target_pairs={{0,8},{8,0},{1,9},{9,1},{2,10},{10,2},{3,11},{11,3},{4,12},{12,4},... | collective-permute-start | bytes 405512 | tf_op jit(solution)/shard_map/ppermute | solution.py:20
where the time goes:
time: 80.1 us; the launch traced here: 79.7 us
  waiting for transfers between devices  29.2 us (36%)
  local copies, waits for them, and re-layouts  24.4 us (30%)
  starting transfers between devices  13.7 us (17%)
  other arithmetic  9.1 us (11%)
  matrix products  2.38 us (3%)
  between operations  0.9 us (1%)
    all_to_all x1, waiting for transfers between devices, local(): lax.all_to_all(ordered, 'sub', split_axis=0, concat_axis=2, tiled=True)  14.9 us
    ppermute x4, waiting for transfers between devices, from_partner(): return lax.ppermute(block, axis, route)  14.4 us
    all_to_all x1, starting transfers between devices, local(): lax.all_to_all(ordered, 'sub', split_axis=0, concat_axis=2, tiled=True)  7.39 us
    ppermute x4, starting transfers between devices, from_partner(): return lax.ppermute(block, axis, route)  6.35 us
    slice x37, local copies, waits for them, and re-layouts, delay_rows(): rolled = jnp.pad(moved[:, offset:], ((0, 0), (0, offset)))  4.93 us
    select_n x28, other arithmetic, delay_rows(): moved = jnp.where(flagged, rolled, moved)  3.93 us
    gather x5, local copies, waits for them, and re-layouts, merge_level(): jnp.take(current, starts + child_rows + entries[1], axis=1 - time_axis)  3.6 us
    gather x5, local copies, waits for them, and re-layouts, merge_level(): lower_rows = jnp.take(current, starts + entries[0], axis=1 - time_axis)  3.59 us
  transfers between devices with their start and end apart: 5, of which 5 were waited for; matrix products, arithmetic and copies ran while one was open for 1% of the time, Pallas kernels for 0%

commit v1 on v0

--- a/solution.py
+++ b/solution.py
@@ -1,8 +1,11 @@
+import functools
 import math
 
 import jax
 import jax.numpy as jnp
 from jax import lax
+from jax.experimental import pallas as pl
+from jax.experimental.pallas import tpu as pltpu
 from jax.sharding import PartitionSpec as P
 
 LOCAL = 5
@@ -132,7 +135,118 @@
     return spectrum(current[:, :SAMPLES], channels)
 
 
+def reversed_bits(values, bits):
+    flipped = jnp.zeros_like(values)
+    for bit_num in range(bits):
+        flipped = flipped | ((values >> bit_num & 1) << (bits - 1 - bit_num))
+    return flipped
+
+
+def one_hot(row_index, depth):
+    rows = lax.broadcasted_iota(jnp.int32, (depth, row_index.shape[1]), 0)
+    return (rows == row_index).astype(jnp.float32).astype(jnp.bfloat16)
+
+
+def merge_kernel(owners, step, order_ref, table_ref, before_ref, own_ref, after_ref, out_ref, joined, current):
+    levels, _, rows = table_ref.shape
+    extra = before_ref.shape[0]
+    window = own_ref.shape[0]
+    length = out_ref.shape[1]
+    whole = length + rows
+    joined[0:extra, :] = before_ref[...]
+    joined[extra : extra + window, :] = own_ref[...]
+    joined[extra + window :, :] = after_ref[...]
+    first = pl.multiple_of(extra - step * lax.axis_index("sub"), step)
+    lanes = lax.broadcasted_iota(jnp.int32, (1, rows), 1)
+    have = whole
+    left = rows
+    for level_num in range(1, levels + 1):
+        child_rows = max(1, 2 ** (level_num - 2))
+        entries = table_ref[level_num - 1]
+        shifts = entries[2:3]
+        if level_num == 1:
+            chosen = one_hot(order_ref[...], order_ref.shape[1])
+            source = joined[pl.ds(first, whole), :]
+        else:
+            starts = 2 * child_rows * (lanes >> (level_num - 1))
+            lower = one_hot(starts + entries[0:1], rows)
+            upper = one_hot(starts + child_rows + entries[1:2], rows)
+            chosen = jnp.concatenate([lower, upper], axis=1)
+            source = current[0:have, :]
+        left -= child_rows
+        keep = -(-(length + left) // 16) * 16
+        picked = jnp.dot(source, chosen, preferred_element_type=jnp.float32)
+        for base in range(0, rows, 128):
+            moved = picked[:, rows + base : rows + base + 128]
+            amounts = shifts[:, base : base + 128]
+            for bit_num in reversed(range(child_rows.bit_length())):
+                size = moved.shape[0]
+                rolled = pltpu.roll(moved, size - 2**bit_num, axis=0)
+                flagged = jnp.broadcast_to(amounts >> bit_num & 1, moved.shape) == 1
+                moved = jnp.where(flagged, rolled, moved)
+                needed = min(size, keep + -(-(2**bit_num - 1) // 8) * 8)
+                moved = moved[0:needed]
+            current[0:keep, base : base + 128] = (
+                picked[0:keep, base : base + 128] + moved[0:keep]
+            ).astype(jnp.bfloat16)
+        have = keep
+    held = rows // owners
+    places = lax.broadcasted_iota(jnp.int32, (rows, rows), 0)
+    shift = held.bit_length() - 1
+    sources = (reversed_bits(places >> shift, owners.bit_length() - 1) << shift) + (places & (held - 1))
+    turned = (lax.broadcasted_iota(jnp.int32, (rows, rows), 1) == sources).astype(jnp.float32)
+    out_ref[...] = lax.dot_general(
+        turned.astype(jnp.bfloat16),
+        current[0:length, :],
+        (((1,), (1,)), ((), ())),
+        preferred_element_type=jnp.float32,
+    ).astype(jnp.bfloat16)
+
+
+def local_sliced(samples, channel_order, merge_table):
+    owners = lax.axis_size("sub")
+    window, channels = samples.shape
+    rows = merge_table.shape[2]
+    length = window - rows // owners
+    step = window - length
+    extra = step * (owners - 1)
+    onward = [(at, at + 1) for at in range(owners - 1)]
+    back = [(at + 1, at) for at in range(owners - 1)]
+    before = lax.ppermute(samples[window - extra :], "sub", onward)
+    after = lax.ppermute(samples[:extra], "sub", back)
+    order = channel_order.reshape(rows, 2).T.reshape(1, channels)
+    vmem = pl.BlockSpec(memory_space=pltpu.VMEM)
+    delays = pl.pallas_call(
+        functools.partial(merge_kernel, owners, step),
+        out_shape=jax.ShapeDtypeStruct((rows, length), jnp.bfloat16),
+        in_specs=[vmem] * 5,
+        out_specs=vmem,
+        scratch_shapes=[
+            pltpu.VMEM((window + 2 * extra, channels), jnp.bfloat16),
+            pltpu.VMEM((length + rows, rows), jnp.bfloat16),
+        ],
+        compiler_params=pltpu.CompilerParams(vmem_limit_bytes=32 * 1024 * 1024),
+        name="merge_rows",
+    )(order, merge_table, before, samples, after)
+    held = rows // owners
+    blocks = lax.all_to_all(delays.reshape(owners, held, length), "sub", 0, 0, tiled=True)
+    series = blocks.transpose(1, 0, 2).reshape(held, owners * length)
+    return spectrum(series, channels)
+
+
+def is_sliced(window, owners, rows):
+    step = rows // owners
+    length = window - step
+    return step % 16 == 0 and length % 128 == 0 and step * (owners - 1) <= window
+
+
+def local_any(samples, channel_order, merge_table):
+    if is_sliced(samples.shape[0], lax.axis_size("sub"), merge_table.shape[2]):
+        return local_sliced(samples, channel_order, merge_table)
+    return local(samples, channel_order, merge_table)
+
+
 def solution(mesh):
     in_specs = (P(("groups", "sub"), None), P(), P())
     out_specs = P(("groups", "sub"), None)
-    return jax.shard_map(local, mesh=mesh, in_specs=in_specs, out_specs=out_specs, check_vma=False)
+    return jax.shard_map(local_any, mesh=mesh, in_specs=in_specs, out_specs=out_specs, check_vma=False)

time: 80.1 us -> 37.4 us (0.47)
  local copies, waits for them, and re-layouts: 24.4 us -> 2.59 us
  waiting for transfers between devices: 29.2 us -> 10.7 us
  other arithmetic: 9.1 us -> 0.15 us
  Pallas kernels: 0 us -> 4.67 us
  starting transfers between devices: 13.7 us -> 16.5 us
    gather x19 -> x0, local copies, waits for them, and re-layouts: 15 us -> none  [the longest x5 3.6 us: merge_level(): jnp.take(current, starts + child_rows + entries[1], axis=1 - time_axis)]
    ppermute x4 -> x2, waiting for transfers between devices: 14.4 us -> 0.85 us  [the longest x1 0.85 us: local_sliced(): before = lax.ppermute(samples[window - extra:], 'sub', onward)]
    select_n x43 -> x0, other arithmetic: 5.99 us -> none  [the longest x28 3.93 us: delay_rows(): moved = jnp.where(flagged, rolled, moved)]
    all_to_all x1, waiting for transfers between devices: 14.9 us -> 9.86 us  [local_sliced(): lax.all_to_all(delays.reshape(owners, held, length), 'sub', 0, 0, tiled=T...]
    all_to_all x1, starting transfers between devices: 7.39 us -> 12.1 us  [local_sliced(): lax.all_to_all(delays.reshape(owners, held, length), 'sub', 0, 0, tiled=T...]
    pallas_call x0 -> x1, Pallas kernels: none -> 4.67 us  [local_sliced(): pl.pallas_call(functools.partial(merge_kernel, owners, step), out_shape=j...]
    slice x38 -> x1, local copies, waits for them, and re-layouts: 4.93 us -> 1.15 us  [local_sliced(): after = lax.ppermute(samples[:extra], 'sub', back)]
    unnamed x6 -> x7, local copies, waits for them, and re-layouts: 2.11 us -> 0.02 us
  transfers between devices with their start and end apart: 5 -> 3, of which waited for: 5 -> 2; matrix products, arithmetic and copies ran while one was open for 1% -> 1% of each run, Pallas kernels for 0% -> 0%
where the time goes in v1:
time: 37.4 us; the launch traced here: 37.1 us
  starting transfers between devices  16.5 us (44%)
  waiting for transfers between devices  10.7 us (29%)
  Pallas kernels  4.67 us (12%)
  local copies, waits for them, and re-layouts  2.59 us (7%)
  matrix products  2.37 us (6%)
    all_to_all x1, starting transfers between devices, local_sliced(): lax.all_to_all(delays.reshape(owners, held, length), 'sub', 0, 0, tiled=T...  12.1 us
    all_to_all x1, waiting for transfers between devices, local_sliced(): lax.all_to_all(delays.reshape(owners, held, length), 'sub', 0, 0, tiled=T...  9.86 us
    pallas_call x1, Pallas kernels, local_sliced(): pl.pallas_call(functools.partial(merge_kernel, owners, step), out_shape=j...  4.67 us
    ppermute x1, starting transfers between devices, local_sliced(): before = lax.ppermute(samples[window - extra:], 'sub', onward)  3.05 us
    ppermute x1, starting transfers between devices, local_sliced(): after = lax.ppermute(samples[:extra], 'sub', back)  1.29 us
    slice x1, local copies, waits for them, and re-layouts, local_sliced(): after = lax.ppermute(samples[:extra], 'sub', back)  1.15 us
    reshape x1, local copies, waits for them, and re-layouts, spectrum(): return power.reshape(row_count, 64 * fold_size)  0.89 us
    ppermute x1, waiting for transfers between devices, local_sliced(): before = lax.ppermute(samples[window - extra:], 'sub', onward)  0.85 us
  transfers between devices with their start and end apart: 3, of which 2 were waited for; matrix products, arithmetic and copies ran while one was open for 1% of the time, Pallas kernels for 0%

profile of v1, /device:TPU:0, one launch (start us, length us, event | category | flops | bytes accessed | tf_op | source)
XLA Modules:
  0.0 37.1 jit_solution(13282759371138899966)
XLA Ops:
  0.0 1.2 %fusion.64 = (bf16[240,512]{1,0:T(8,128)(2,1)S(1)}, bf16[240,512]{1,0:T(8,128)(2,1)S(1)}) fusion(bf16[528,512]{1,0:T(8,128)(2,1)} %own_ref.1), kind=kLoop, calls=%fused_computation.75 | loop fusion | bytes 983040 | tf_op jit(solution)/shard_map/slice | solution.py:216
  1.2 0.0 copy-start.2
  1.2 1.3 %collective-permute-start.1 = (bf16[240,512]{1,0:T(8,128)(2,1)S(1)}, bf16[240,512]{1,0:T(8,128)(2,1)S(1)}, u32[]{:S(2)}, u32[]{:S(2)}) collective-permute-start(bf16[240,512]{1,0:T(8,128)(2,1)S(1)} %get-tuple-element.7), channel_id=1, source_target_pairs={{1,0},{2,1},{3,2},{4,3},{5,4},{6,5},{7,6},{8,7},{9,8},{10,9},{11,1... | collective-permute-start | bytes 737288 | tf_op jit(solution)/shard_map/ppermute | solution.py:216
  2.5 3.0 %collective-permute-start = (bf16[240,512]{1,0:T(8,128)(2,1)S(1)}, bf16[240,512]{1,0:T(8,128)(2,1)S(1)}, u32[]{:S(2)}, u32[]{:S(2)}) collective-permute-start(bf16[240,512]{1,0:T(8,128)(2,1)S(1)} %get-tuple-element.8), channel_id=1, source_target_pairs={{0,1},{1,2},{2,3},{3,4},{4,5},{5,6},{6,7},{7,8},{8,9},{9,10},{10,1... | collective-permute-start | bytes 737288 | tf_op jit(solution)/shard_map/ppermute | solution.py:215
  5.5 0.0 copy-done.2
  5.5 0.1 reshape.48
  5.7 0.0 copy-start.1
  5.7 0.1 copy.5
  5.8 0.0 collective-permute-done.1.after_ref
  5.8 0.9 %collective-permute-done.before_ref = bf16[240,512]{1,0:T(8,128)(2,1)S(1)} collective-permute-done((bf16[240,512]{1,0:T(8,128)(2,1)S(1)}, bf16[240,512]{1,0:T(8,128)(2,1)S(1)}, u32[]{:S(2)}, u32[]{:S(2)}) %collective-permute-start) | collective-permute-done | bytes 245792 | tf_op jit(solution)/shard_map/ppermute | solution.py:215
  6.6 0.0 copy-done
  6.6 4.7 %merge_rows.1 = bf16[256,512]{1,0:T(8,128)(2,1)} custom-call(s32[1,512]{1,0:T(1,128)S(1)} %bitcast.34, s32[9,3,256]{2,1,0:T(4,128)S(1)} %copy-done.1, bf16[240,512]{1,0:T(8,128)(2,1)S(1)} %collective-permute-done.before_ref, bf16[528,512]{1,0:T(8,128)(2,1)S(1)} %copy-done, bf16[240,512]{1,0:T(8,128)(2,1)S(1)} %collective-permute-done.1.after_ref), custom_call_target="tpu_custom_call" | custom-call | tf_op jit(solution)/shard_map/merge_rows/pallas_call | solution.py:219
  11.3 12.1 %all-to-all-start = ((bf16[16,16,512]{2,1,0:T(8,128)(2,1)}), bf16[16,16,512]{2,1,0:T(8,128)(2,1)S(1)}, u32[]{:S(2)}, u32[]{:S(2)}) async-start(bf16[16,16,512]{2,1,0:T(8,128)(2,1)} %bitcast.2), calls=%async_computation | async-start | bytes 524288 | tf_op jit(solution)/shard_map/all_to_all | solution.py:232
  23.4 0.1 fusion.30
  23.6 9.9 %all-to-all-done = bf16[16,16,512]{2,1,0:T(8,128)(2,1)S(1)} async-done(((bf16[16,16,512]{2,1,0:T(8,128)(2,1)}), bf16[16,16,512]{2,1,0:T(8,128)(2,1)S(1)}, u32[]{:S(2)}, u32[]{:S(2)}) %all-to-all-start) | async-done | bytes 262176 | tf_op jit(solution)/shard_map/all_to_all | solution.py:232
  33.5 0.1 copy.6
  33.6 0.2 reshape_reshape.3
  33.8 0.3 convolution_bitcast_fusion
  34.1 0.4 %add_convert_fusion = (bf16[16,64,128]{2,1,0:T(8,128)(2,1)S(1)}, bf16[16,64,128]{2,1,0:T(8,128)(2,1)S(1)}) fusion(f32[16,64,128]{2,1,0:T(8,128)S(1)} %convolution_bitcast_fusion, f32[64,128]{1,0:T(8,128)S(1)} %get-tuple-element.9, f32[64,128]{1,0:T(8,128)S(1)} %get-tuple-element.10, bf16[16,64,128]{2,1,0:T(8,128)(2,1)S(1)} %reshape_reshape.3), kind=kOutput, calls=%fused_computation.11 | convolution fusion | flops 18018304 | bytes 1376256 | tf_op jit(solution)/shard_map/kn,rnm->rkm/dot_general | solution.py:77
  34.5 0.4 %fusion.38 = f32[64,16,64]{2,0,1:T(8,128)S(1)} fusion(bf16[16,64,128]{2,1,0:T(8,128)(2,1)S(1)} %get-tuple-element.5), kind=kOutput, calls=%fused_computation.50 | convolution fusion | flops 16900096 | bytes 524288 | tf_op jit(solution)/shard_map/rkn,nj->rjk/dot_general | solution.py:80
  34.9 0.4 %fusion.36 = f32[64,16,64]{2,0,1:T(8,128)S(1)} fusion(bf16[16,64,128]{2,1,0:T(8,128)(2,1)S(1)} %get-tuple-element.6), kind=kOutput, calls=%fused_computation.49 | convolution fusion | flops 16900096 | bytes 524288 | tf_op jit(solution)/shard_map/rkn,nj->rjk/dot_general | solution.py:83
  35.3 0.4 %fusion.1 = f32[64,16,64]{2,0,1:T(8,128)S(1)} fusion(f32[64,16,64]{2,0,1:T(8,128)S(1)} %fusion.36, bf16[16,64,128]{2,1,0:T(8,128)(2,1)S(1)} %get-tuple-element.5), kind=kOutput, calls=%fused_computation.4 | convolution fusion | flops 17031168 | bytes 786432 | tf_op jit(solution)/shard_map/rkn,nj->rjk/dot_general | solution.py:85
  35.8 0.4 %fusion.5 = f32[16,64,64]{2,1,0:T(8,128)S(1)} fusion(f32[64,16,64]{2,0,1:T(8,128)S(1)} %fusion.1, f32[64,16,64]{2,0,1:T(8,128)S(1)} %fusion.38, bf16[16,64,128]{2,1,0:T(8,128)(2,1)S(1)} %get-tuple-element.6), kind=kOutput, calls=%fused_computation.9 | convolution fusion | flops 17162240 | bytes 1048576 | tf_op jit(solution)/shard_map/rkn,nj->rjk/dot_general | solution.py:82
  36.2 0.9 %reshape.51 = f32[16,4096]{1,0:T(8,128)} reshape(f32[16,64,64]{2,1,0:T(8,128)S(1)} %fusion.5) | data formatting | bytes 524288 | tf_op jit(solution)/shard_map/reshape | solution.py:87
  (3 shorter events, 0.0 us)
Async XLA Ops:
  0.0 6.6 %copy-start = (bf16[528,512]{1,0:T(8,128)(2,1)S(1)}, bf16[528,512]{1,0:T(8,128)(2,1)}, u32[]{:S(2)}) copy-start(bf16[528,512]{1,0:T(8,128)(2,1)} %own_ref.1) | copy-start | bytes 1622020
  1.2 4.4 %copy-start.2 = (s32[512]{0:T(512)S(1)}, s32[512]{0:T(512)}, u32[]{:S(2)}) copy-start(s32[512]{0:T(512)} %param.4) | copy-start | bytes 6148
  1.2 4.6 %collective-permute-start.1 = (bf16[240,512]{1,0:T(8,128)(2,1)S(1)}, bf16[240,512]{1,0:T(8,128)(2,1)S(1)}, u32[]{:S(2)}, u32[]{:S(2)}) collective-permute-start(bf16[240,512]{1,0:T(8,128)(2,1)S(1)} %get-tuple-element.7), channel_id=1, source_target_pairs={{1,0},{2,1},{3,2},{4,3},{5,4},{6,5},{7,6},{8,7},{9,8},{10,9},{11,1... | collective-permute-start | bytes 737288 | tf_op jit(solution)/shard_map/ppermute | solution.py:216
  2.5 4.2 %collective-permute-start = (bf16[240,512]{1,0:T(8,128)(2,1)S(1)}, bf16[240,512]{1,0:T(8,128)(2,1)S(1)}, u32[]{:S(2)}, u32[]{:S(2)}) collective-permute-start(bf16[240,512]{1,0:T(8,128)(2,1)S(1)} %get-tuple-element.8), channel_id=1, source_target_pairs={{0,1},{1,2},{2,3},{3,4},{4,5},{5,6},{6,7},{7,8},{8,9},{9,10},{10,1... | collective-permute-start | bytes 737288 | tf_op jit(solution)/shard_map/ppermute | solution.py:215
  5.7 1.0 %copy-start.1 = (s32[9,3,256]{2,1,0:T(4,128)S(1)}, s32[9,3,256]{2,1,0:T(4,128)}, u32[]{:S(2)}) copy-start(s32[9,3,256]{2,1,0:T(4,128)} %table_ref.1) | copy-start | bytes 82948
  11.3 22.2 %all-to-all-start = ((bf16[16,16,512]{2,1,0:T(8,128)(2,1)}), bf16[16,16,512]{2,1,0:T(8,128)(2,1)S(1)}, u32[]{:S(2)}, u32[]{:S(2)}) async-start(bf16[16,16,512]{2,1,0:T(8,128)(2,1)} %bitcast.2), calls=%async_computation | async-start | bytes 524288 | tf_op jit(solution)/shard_map/all_to_all | solution.py:232

commit v2 on v1

--- a/solution.py
+++ b/solution.py
@@ -9,6 +9,7 @@
 from jax.sharding import PartitionSpec as P
 
 LOCAL = 5
+MESH = pl.DeviceIdType.MESH
 CH_DEV = 32
 SAMPLES = 8192
 
@@ -147,31 +148,93 @@
     return (rows == row_index).astype(jnp.float32).astype(jnp.bfloat16)
 
 
-def merge_kernel(owners, step, order_ref, table_ref, before_ref, own_ref, after_ref, out_ref, joined, current):
+def merge_kernel(
+    owners,
+    step,
+    order_ref,
+    table_ref,
+    own_ref,
+    out_ref,
+    joined,
+    current,
+    picks,
+    first_pick,
+    turned,
+    halo_send,
+    halo_recv,
+    block_send,
+    block_recv,
+):
     levels, _, rows = table_ref.shape
-    extra = before_ref.shape[0]
+    extra = step * (owners - 1)
     window = own_ref.shape[0]
-    length = out_ref.shape[1]
+    _, held, length = out_ref.shape
     whole = length + rows
-    joined[0:extra, :] = before_ref[...]
+    me = lax.axis_index("sub")
+
+    barrier = pltpu.get_barrier_semaphore()
+    for apart in range(1, owners):
+        pl.semaphore_signal(
+            barrier, inc=1, device_id={"sub": lax.rem(me + apart, owners)}, device_id_type=MESH
+        )
     joined[extra : extra + window, :] = own_ref[...]
-    joined[extra + window :, :] = after_ref[...]
-    first = pl.multiple_of(extra - step * lax.axis_index("sub"), step)
+    first_pick[...] = one_hot(order_ref[...], order_ref.shape[1])
+    pl.semaphore_wait(barrier, owners - 1)
+
+    onward = pltpu.make_async_remote_copy(
+        src_ref=own_ref.at[window - extra :],
+        dst_ref=joined.at[0:extra],
+        send_sem=halo_send.at[0],
+        recv_sem=halo_recv.at[0],
+        device_id={"sub": lax.rem(me + 1, owners)},
+        device_id_type=MESH,
+    )
+    back = pltpu.make_async_remote_copy(
+        src_ref=own_ref.at[0:extra],
+        dst_ref=joined.at[extra + window :],
+        send_sem=halo_send.at[1],
+        recv_sem=halo_recv.at[1],
+        device_id={"sub": lax.rem(me + owners - 1, owners)},
+        device_id_type=MESH,
+    )
+
+    @pl.when(me < owners - 1)
+    def _():
+        onward.start()
+
+    @pl.when(me > 0)
+    def _():
+        back.start()
+
     lanes = lax.broadcasted_iota(jnp.int32, (1, rows), 1)
+    for level_num in range(2, levels + 1):
+        child_rows = max(1, 2 ** (level_num - 2))
+        entries = table_ref[level_num - 1]
+        starts = 2 * child_rows * (lanes >> (level_num - 1))
+        picks[level_num - 2, :, 0:rows] = one_hot(starts + entries[0:1], rows)
+        picks[level_num - 2, :, rows:] = one_hot(starts + child_rows + entries[1:2], rows)
+
+    @pl.when(me < owners - 1)
+    def _():
+        onward.wait_send()
+        back.wait_recv()
+
+    @pl.when(me > 0)
+    def _():
+        back.wait_send()
+        onward.wait_recv()
+
+    first = pl.multiple_of(extra - step * me, step)
     have = whole
     left = rows
     for level_num in range(1, levels + 1):
         child_rows = max(1, 2 ** (level_num - 2))
-        entries = table_ref[level_num - 1]
-        shifts = entries[2:3]
+        shifts = table_ref[level_num - 1][2:3]
         if level_num == 1:
-            chosen = one_hot(order_ref[...], order_ref.shape[1])
+            chosen = first_pick[...]
             source = joined[pl.ds(first, whole), :]
         else:
-            starts = 2 * child_rows * (lanes >> (level_num - 1))
-            lower = one_hot(starts + entries[0:1], rows)
-            upper = one_hot(starts + child_rows + entries[1:2], rows)
-            chosen = jnp.concatenate([lower, upper], axis=1)
+            chosen = picks[level_num - 2]
             source = current[0:have, :]
         left -= child_rows
         keep = -(-(length + left) // 16) * 16
@@ -190,46 +253,66 @@
                 picked[0:keep, base : base + 128] + moved[0:keep]
             ).astype(jnp.bfloat16)
         have = keep
-    held = rows // owners
     places = lax.broadcasted_iota(jnp.int32, (rows, rows), 0)
     shift = held.bit_length() - 1
     sources = (reversed_bits(places >> shift, owners.bit_length() - 1) << shift) + (places & (held - 1))
-    turned = (lax.broadcasted_iota(jnp.int32, (rows, rows), 1) == sources).astype(jnp.float32)
-    out_ref[...] = lax.dot_general(
-        turned.astype(jnp.bfloat16),
+    placed = (lax.broadcasted_iota(jnp.int32, (rows, rows), 1) == sources).astype(jnp.float32)
+    turned[...] = lax.dot_general(
+        placed.astype(jnp.bfloat16),
         current[0:length, :],
         (((1,), (1,)), ((), ())),
         preferred_element_type=jnp.float32,
     ).astype(jnp.bfloat16)
 
+    copies = []
+    for apart in range(1, owners):
+        target = lax.rem(me + apart, owners)
+        copy = pltpu.make_async_remote_copy(
+            src_ref=turned.at[pl.ds(pl.multiple_of(target * held, held), held)],
+            dst_ref=out_ref.at[me],
+            send_sem=block_send.at[apart],
+            recv_sem=block_recv.at[apart],
+            device_id={"sub": target},
+            device_id_type=MESH,
+        )
+        copy.start()
+        copies.append(copy)
+    out_ref[me] = turned[pl.ds(pl.multiple_of(me * held, held), held), :]
+    for copy in copies:
+        copy.wait()
+
 
 def local_sliced(samples, channel_order, merge_table):
     owners = lax.axis_size("sub")
     window, channels = samples.shape
-    rows = merge_table.shape[2]
-    length = window - rows // owners
+    levels, _, rows = merge_table.shape
+    held = rows // owners
+    length = window - held
     step = window - length
     extra = step * (owners - 1)
-    onward = [(at, at + 1) for at in range(owners - 1)]
-    back = [(at + 1, at) for at in range(owners - 1)]
-    before = lax.ppermute(samples[window - extra :], "sub", onward)
-    after = lax.ppermute(samples[:extra], "sub", back)
     order = channel_order.reshape(rows, 2).T.reshape(1, channels)
     vmem = pl.BlockSpec(memory_space=pltpu.VMEM)
-    delays = pl.pallas_call(
+    blocks = pl.pallas_call(
         functools.partial(merge_kernel, owners, step),
-        out_shape=jax.ShapeDtypeStruct((rows, length), jnp.bfloat16),
-        in_specs=[vmem] * 5,
+        out_shape=jax.ShapeDtypeStruct((owners, held, length), jnp.bfloat16),
+        in_specs=[vmem] * 3,
         out_specs=vmem,
         scratch_shapes=[
             pltpu.VMEM((window + 2 * extra, channels), jnp.bfloat16),
             pltpu.VMEM((length + rows, rows), jnp.bfloat16),
+            pltpu.VMEM((levels - 1, rows, 2 * rows), jnp.bfloat16),
+            pltpu.VMEM((channels, channels), jnp.bfloat16),
+            pltpu.VMEM((rows, length), jnp.bfloat16),
+            pltpu.SemaphoreType.DMA((2,)),
+            pltpu.SemaphoreType.DMA((2,)),
+            pltpu.SemaphoreType.DMA((owners,)),
+            pltpu.SemaphoreType.DMA((owners,)),
         ],
-        compiler_params=pltpu.CompilerParams(vmem_limit_bytes=32 * 1024 * 1024),
+        compiler_params=pltpu.CompilerParams(
+            vmem_limit_bytes=32 * 1024 * 1024, collective_id=0, has_side_effects=True
+        ),
         name="merge_rows",
-    )(order, merge_table, before, samples, after)
-    held = rows // owners
-    blocks = lax.all_to_all(delays.reshape(owners, held, length), "sub", 0, 0, tiled=True)
+    )(order, merge_table, samples)
     series = blocks.transpose(1, 0, 2).reshape(held, owners * length)
     return spectrum(series, channels)
 

time: 37.4 us -> 27.4 us (0.73)
  starting transfers between devices: 16.5 us -> 0 us
  Pallas kernels: 4.67 us -> 20.7 us
  waiting for transfers between devices: 10.7 us -> 0 us
  local copies, waits for them, and re-layouts: 2.59 us -> 3.83 us
    pallas_call x1, Pallas kernels: 4.67 us -> 20.7 us  [local_sliced(): pl.pallas_call(functools.partial(merge_kernel, owners, step), out_shape=j...]
    all_to_all x1 -> x0, starting transfers between devices: 12.1 us -> none  [local_sliced(): lax.all_to_all(delays.reshape(owners, held, length), 'sub', 0, 0, tiled=T...]
    all_to_all x1 -> x0, waiting for transfers between devices: 9.86 us -> none  [local_sliced(): lax.all_to_all(delays.reshape(owners, held, length), 'sub', 0, 0, tiled=T...]
    ppermute x2 -> x0, starting transfers between devices: 4.34 us -> none  [the longest x1 3.05 us: local_sliced(): before = lax.ppermute(samples[window - extra:], 'sub', onward)]
    unnamed x7, local copies, waits for them, and re-layouts: 0.02 us -> 2.41 us
    slice x1 -> x0, local copies, waits for them, and re-layouts: 1.15 us -> none  [local_sliced(): after = lax.ppermute(samples[:extra], 'sub', back)]
    ppermute x2 -> x0, waiting for transfers between devices: 0.85 us -> none  [the longest x1 0.85 us: local_sliced(): before = lax.ppermute(samples[window - extra:], 'sub', onward)]
  transfers between devices with their start and end apart: 3 -> 0, of which waited for: 2 -> 0; matrix products, arithmetic and copies ran while one was open for 1% -> 0% of each run, Pallas kernels for 0% -> 0%
where the time goes in v2:
time: 27.4 us; the launch traced here: 27.2 us
  Pallas kernels  20.7 us (76%)
  local copies, waits for them, and re-layouts  3.83 us (14%)
  matrix products  2.37 us (9%)
    pallas_call x1, Pallas kernels, local_sliced(): pl.pallas_call(functools.partial(merge_kernel, owners, step), out_shape=j...  20.7 us
    unnamed x7, local copies, waits for them, and re-layouts  2.41 us
    reshape x1, local copies, waits for them, and re-layouts, spectrum(): return power.reshape(row_count, 64 * fold_size)  0.89 us

profile of v2, /device:TPU:0, one launch (start us, length us, event | category | flops | bytes accessed | tf_op | source)
XLA Modules:
  0.0 27.2 jit_solution(15173999218819602945)
XLA Ops:
  0.0 0.1 fusion.30
  0.1 0.0 copy-start.2
  0.2 0.7 %copy-done.2 = s32[512]{0:T(512)S(1)} copy-done((s32[512]{0:T(512)S(1)}, s32[512]{0:T(512)}, u32[]{:S(2)}) %copy-start.2) | copy-done | bytes 2072
  0.8 0.1 reshape.45
  1.0 0.0 copy-start.1
  1.0 0.1 copy.4
  1.1 0.7 %copy-done.1 = s32[9,3,256]{2,1,0:T(4,128)S(1)} copy-done((s32[9,3,256]{2,1,0:T(4,128)S(1)}, s32[9,3,256]{2,1,0:T(4,128)}, u32[]{:S(2)}) %copy-start.1) | copy-done | bytes 27672
  1.7 0.0 copy-start
  1.8 1.0 %copy-done = bf16[528,512]{1,0:T(8,128)(2,1)S(1)} copy-done((bf16[528,512]{1,0:T(8,128)(2,1)S(1)}, bf16[528,512]{1,0:T(8,128)(2,1)}, u32[]{:S(2)}) %copy-start) | copy-done | bytes 540696
  2.8 20.7 %merge_rows.1 = bf16[16,16,512]{2,1,0:T(8,128)(2,1)S(1)} custom-call(s32[1,512]{1,0:T(1,128)S(1)} %bitcast.34, s32[9,3,256]{2,1,0:T(4,128)S(1)} %copy-done.1, bf16[528,512]{1,0:T(8,128)(2,1)S(1)} %copy-done), custom_call_target="tpu_custom_call" | custom-call | tf_op jit(solution)/shard_map/merge_rows/pallas_call | solution.py:295
  23.5 0.2 copy.5
  23.7 0.2 reshape_reshape.3
  23.9 0.3 %convolution_bitcast_fusion = f32[16,64,128]{2,1,0:T(8,128)S(1)} fusion(bf16[16,64,128]{2,1,0:T(8,128)(2,1)S(1)} %reshape_reshape.3), kind=kOutput, calls=%fused_computation.2 | convolution fusion | flops 16838656 | bytes 786432 | tf_op jit(solution)/shard_map/kn,rnm->rkm/dot_general | solution.py:77
  24.2 0.4 %add_convert_fusion = (bf16[16,64,128]{2,1,0:T(8,128)(2,1)S(1)}, bf16[16,64,128]{2,1,0:T(8,128)(2,1)S(1)}) fusion(f32[16,64,128]{2,1,0:T(8,128)S(1)} %convolution_bitcast_fusion, f32[64,128]{1,0:T(8,128)S(1)} %get-tuple-element.7, f32[64,128]{1,0:T(8,128)S(1)} %get-tuple-element.8, bf16[16,64,128]{2,1,0:T(8,128)(2,1)S(1)} %reshape_reshape.3), kind=kOutput, calls=%fused_computation.11 | convolution fusion | flops 18018304 | bytes 1376256 | tf_op jit(solution)/shard_map/kn,rnm->rkm/dot_general | solution.py:78
  24.6 0.4 %fusion.38 = f32[64,16,64]{2,0,1:T(8,128)S(1)} fusion(bf16[16,64,128]{2,1,0:T(8,128)(2,1)S(1)} %get-tuple-element.5), kind=kOutput, calls=%fused_computation.50 | convolution fusion | flops 16900096 | bytes 524288 | tf_op jit(solution)/shard_map/rkn,nj->rjk/dot_general | solution.py:81
  25.0 0.4 %fusion.36 = f32[64,16,64]{2,0,1:T(8,128)S(1)} fusion(bf16[16,64,128]{2,1,0:T(8,128)(2,1)S(1)} %get-tuple-element.6), kind=kOutput, calls=%fused_computation.49 | convolution fusion | flops 16900096 | bytes 524288 | tf_op jit(solution)/shard_map/rkn,nj->rjk/dot_general | solution.py:84
  25.4 0.4 %fusion.1 = f32[64,16,64]{2,0,1:T(8,128)S(1)} fusion(f32[64,16,64]{2,0,1:T(8,128)S(1)} %fusion.36, bf16[16,64,128]{2,1,0:T(8,128)(2,1)S(1)} %get-tuple-element.5), kind=kOutput, calls=%fused_computation.4 | convolution fusion | flops 17031168 | bytes 786432 | tf_op jit(solution)/shard_map/rkn,nj->rjk/dot_general | solution.py:86
  25.8 0.4 %fusion.5 = f32[16,64,64]{2,1,0:T(8,128)S(1)} fusion(f32[64,16,64]{2,0,1:T(8,128)S(1)} %fusion.1, f32[64,16,64]{2,0,1:T(8,128)S(1)} %fusion.38, bf16[16,64,128]{2,1,0:T(8,128)(2,1)S(1)} %get-tuple-element.6), kind=kOutput, calls=%fused_computation.9 | convolution fusion | flops 17162240 | bytes 1048576 | tf_op jit(solution)/shard_map/rkn,nj->rjk/dot_general | solution.py:83
  26.3 0.9 %reshape.47 = f32[16,4096]{1,0:T(8,128)} reshape(f32[16,64,64]{2,1,0:T(8,128)S(1)} %fusion.5) | data formatting | bytes 524288 | tf_op jit(solution)/shard_map/reshape | solution.py:88
  (1 shorter events, 0.0 us)
Async XLA Ops:
  0.1 0.7 %copy-start.2 = (s32[512]{0:T(512)S(1)}, s32[512]{0:T(512)}, u32[]{:S(2)}) copy-start(s32[512]{0:T(512)} %param.4) | copy-start | bytes 6148
  1.0 0.8 %copy-start.1 = (s32[9,3,256]{2,1,0:T(4,128)S(1)}, s32[9,3,256]{2,1,0:T(4,128)}, u32[]{:S(2)}) copy-start(s32[9,3,256]{2,1,0:T(4,128)} %table_ref.1) | copy-start | bytes 82948
  1.7 1.0 %copy-start = (bf16[528,512]{1,0:T(8,128)(2,1)S(1)}, bf16[528,512]{1,0:T(8,128)(2,1)}, u32[]{:S(2)}) copy-start(bf16[528,512]{1,0:T(8,128)(2,1)} %own_ref.1) | copy-start | bytes 1622020

commit v3 on v2

--- a/solution.py
+++ b/solution.py
@@ -151,10 +151,12 @@
 def merge_kernel(
     owners,
     step,
+    order_hbm,
+    table_hbm,
+    own_ref,
+    out_ref,
     order_ref,
     table_ref,
-    own_ref,
-    out_ref,
     joined,
     current,
     picks,
@@ -164,6 +166,7 @@
     halo_recv,
     block_send,
     block_recv,
+    load_sem,
 ):
     levels, _, rows = table_ref.shape
     extra = step * (owners - 1)
@@ -172,13 +175,27 @@
     whole = length + rows
     me = lax.axis_index("sub")
 
+    loads = [
+        pltpu.make_async_copy(order_hbm, order_ref, load_sem.at[0]),
+        pltpu.make_async_copy(table_hbm, table_ref, load_sem.at[1]),
+        pltpu.make_async_copy(own_ref, joined.at[extra : extra + window], load_sem.at[2]),
+    ]
+    for load in loads:
+        load.start()
     barrier = pltpu.get_barrier_semaphore()
     for apart in range(1, owners):
         pl.semaphore_signal(
             barrier, inc=1, device_id={"sub": lax.rem(me + apart, owners)}, device_id_type=MESH
         )
-    joined[extra : extra + window, :] = own_ref[...]
-    first_pick[...] = one_hot(order_ref[...], order_ref.shape[1])
+    loads[0].wait()
+    channels = order_ref.shape[1]
+    column = lax.broadcasted_iota(jnp.int32, (1, channels), 1)
+    split = jnp.where(column < rows, 2 * column, 2 * (column - rows) + 1)
+    first_pick[...] = jnp.dot(
+        one_hot(order_ref[...], channels),
+        one_hot(split, channels),
+        preferred_element_type=jnp.float32,
+    ).astype(jnp.bfloat16)
     pl.semaphore_wait(barrier, owners - 1)
 
     onward = pltpu.make_async_remote_copy(
@@ -206,6 +223,7 @@
     def _():
         back.start()
 
+    loads[1].wait()
     lanes = lax.broadcasted_iota(jnp.int32, (1, rows), 1)
     for level_num in range(2, levels + 1):
         child_rows = max(1, 2 ** (level_num - 2))
@@ -224,6 +242,7 @@
         back.wait_send()
         onward.wait_recv()
 
+    loads[2].wait()
     first = pl.multiple_of(extra - step * me, step)
     have = whole
     left = rows
@@ -290,14 +309,16 @@
     length = window - held
     step = window - length
     extra = step * (owners - 1)
-    order = channel_order.reshape(rows, 2).T.reshape(1, channels)
+    order = channel_order.reshape(1, channels)
     vmem = pl.BlockSpec(memory_space=pltpu.VMEM)
     blocks = pl.pallas_call(
         functools.partial(merge_kernel, owners, step),
         out_shape=jax.ShapeDtypeStruct((owners, held, length), jnp.bfloat16),
-        in_specs=[vmem] * 3,
+        in_specs=[pl.BlockSpec(memory_space=pl.ANY)] * 3,
         out_specs=vmem,
         scratch_shapes=[
+            pltpu.VMEM((1, channels), jnp.int32),
+            pltpu.VMEM((levels, 3, rows), jnp.int32),
             pltpu.VMEM((window + 2 * extra, channels), jnp.bfloat16),
             pltpu.VMEM((length + rows, rows), jnp.bfloat16),
             pltpu.VMEM((levels - 1, rows, 2 * rows), jnp.bfloat16),
@@ -307,9 +328,10 @@
             pltpu.SemaphoreType.DMA((2,)),
             pltpu.SemaphoreType.DMA((owners,)),
             pltpu.SemaphoreType.DMA((owners,)),
+            pltpu.SemaphoreType.DMA((3,)),
         ],
         compiler_params=pltpu.CompilerParams(
-            vmem_limit_bytes=32 * 1024 * 1024, collective_id=0, has_side_effects=True
+            vmem_limit_bytes=62 * 1024 * 1024, collective_id=0, has_side_effects=True
         ),
         name="merge_rows",
     )(order, merge_table, samples)

time: 27.4 us -> 26.8 us (0.978)
  local copies, waits for them, and re-layouts: 3.83 us -> 2.16 us
  Pallas kernels: 20.7 us -> 21.9 us
    unnamed x7 -> x0, local copies, waits for them, and re-layouts: 2.41 us -> none
    pallas_call x1, Pallas kernels: 20.7 us -> 21.9 us  [local_sliced(): pl.pallas_call(functools.partial(merge_kernel, owners, step), out_shape=j...]
    transpose x1, local copies, waits for them, and re-layouts: 0.15 us -> 1.1 us  [local_sliced(): series = blocks.transpose(1, 0, 2).reshape(held, owners * length)]
where the time goes in v3:
time: 26.8 us; the launch traced here: 26.7 us
  Pallas kernels  21.9 us (82%)
  matrix products  2.38 us (9%)
  local copies, waits for them, and re-layouts  2.16 us (8%)
    pallas_call x1, Pallas kernels, local_sliced(): pl.pallas_call(functools.partial(merge_kernel, owners, step), out_shape=j...  21.9 us
    transpose x1, local copies, waits for them, and re-layouts, local_sliced(): series = blocks.transpose(1, 0, 2).reshape(held, owners * length)  1.1 us
    reshape x1, local copies, waits for them, and re-layouts, spectrum(): return power.reshape(row_count, 64 * fold_size)  0.89 us

profile of v3, /device:TPU:0, one launch (start us, length us, event | category | flops | bytes accessed | tf_op | source)
XLA Modules:
  0.0 26.7 jit_solution(5361278260538686356)
XLA Ops:
  0.0 0.1 fusion.30
  0.1 21.9 %merge_rows.1 = bf16[16,16,512]{2,1,0:T(8,128)(2,1)} custom-call(s32[1,512]{1,0:T(1,128)} %bitcast.31, s32[9,3,256]{2,1,0:T(4,128)} %table_hbm.1, bf16[528,512]{1,0:T(8,128)(2,1)} %own_ref.1), custom_call_target="tpu_custom_call" | custom-call | tf_op jit(solution)/shard_map/merge_rows/pallas_call | solution.py:314
  22.1 1.1 %copy.4 = bf16[16,16,512]{2,1,0:T(8,128)(2,1)S(1)} copy(bf16[16,16,512]{2,0,1:T(8,128)(2,1)} %bitcast.30) | data formatting | bytes 524288 | tf_op jit(solution)/shard_map/transpose | solution.py:338
  23.2 0.2 reshape_reshape.3
  23.4 0.3 %convolution_bitcast_fusion = f32[16,64,128]{2,1,0:T(8,128)S(1)} fusion(bf16[16,64,128]{2,1,0:T(8,128)(2,1)S(1)} %reshape_reshape.3), kind=kOutput, calls=%fused_computation.2 | convolution fusion | flops 16838656 | bytes 786432 | tf_op jit(solution)/shard_map/kn,rnm->rkm/dot_general | solution.py:77
  23.7 0.4 %add_convert_fusion = (bf16[16,64,128]{2,1,0:T(8,128)(2,1)S(1)}, bf16[16,64,128]{2,1,0:T(8,128)(2,1)S(1)}) fusion(f32[16,64,128]{2,1,0:T(8,128)S(1)} %convolution_bitcast_fusion, f32[64,128]{1,0:T(8,128)S(1)} %get-tuple-element.7, f32[64,128]{1,0:T(8,128)S(1)} %get-tuple-element.8, bf16[16,64,128]{2,1,0:T(8,128)(2,1)S(1)} %reshape_reshape.3), kind=kOutput, calls=%fused_computation.11 | convolution fusion | flops 18018304 | bytes 1376256 | tf_op jit(solution)/shard_map/kn,rnm->rkm/dot_general | solution.py:78
  24.1 0.4 %fusion.38 = f32[64,16,64]{2,0,1:T(8,128)S(1)} fusion(bf16[16,64,128]{2,1,0:T(8,128)(2,1)S(1)} %get-tuple-element.5), kind=kOutput, calls=%fused_computation.50 | convolution fusion | flops 16900096 | bytes 524288 | tf_op jit(solution)/shard_map/rkn,nj->rjk/dot_general | solution.py:81
  24.5 0.4 %fusion.36 = f32[64,16,64]{2,0,1:T(8,128)S(1)} fusion(bf16[16,64,128]{2,1,0:T(8,128)(2,1)S(1)} %get-tuple-element.6), kind=kOutput, calls=%fused_computation.49 | convolution fusion | flops 16900096 | bytes 524288 | tf_op jit(solution)/shard_map/rkn,nj->rjk/dot_general | solution.py:84
  24.9 0.4 %fusion.1 = f32[64,16,64]{2,0,1:T(8,128)S(1)} fusion(f32[64,16,64]{2,0,1:T(8,128)S(1)} %fusion.36, bf16[16,64,128]{2,1,0:T(8,128)(2,1)S(1)} %get-tuple-element.5), kind=kOutput, calls=%fused_computation.4 | convolution fusion | flops 17031168 | bytes 786432 | tf_op jit(solution)/shard_map/rkn,nj->rjk/dot_general | solution.py:86
  25.3 0.4 %fusion.5 = f32[16,64,64]{2,1,0:T(8,128)S(1)} fusion(f32[64,16,64]{2,0,1:T(8,128)S(1)} %fusion.1, f32[64,16,64]{2,0,1:T(8,128)S(1)} %fusion.38, bf16[16,64,128]{2,1,0:T(8,128)(2,1)S(1)} %get-tuple-element.6), kind=kOutput, calls=%fused_computation.9 | convolution fusion | flops 17162240 | bytes 1048576 | tf_op jit(solution)/shard_map/rkn,nj->rjk/dot_general | solution.py:83
  25.8 0.9 %reshape.43 = f32[16,4096]{1,0:T(8,128)} reshape(f32[16,64,64]{2,1,0:T(8,128)S(1)} %fusion.5) | data formatting | bytes 524288 | tf_op jit(solution)/shard_map/reshape | solution.py:88
